TPU v7x, 128 devices: a whole 4x4x4 slice. The times are simulated.
128 devices in a mesh: dp: 16 (over y_lo, z, core), tensor: 8 (over x, y_hi).
Axes of the slice: x: 4, y: 4 (y_hi: 2, y_lo: 2; y = y_hi * 2 + y_lo), z: 4, core: 2. Of those that a mesh axis runs over, the one named last changes fastest.
Arguments:
- hidden_in: float32 [20480, 1024], P(('dp', 'tensor')), may hold values from -6 to 6
- w_qkv: bfloat16 [1024, 2, 3, 1024], P('dp', None, None, 'tensor'), may hold values from -0.1875 to 0.1875
- w_attn_out: bfloat16 [1024, 2, 1024], P('dp', None, 'tensor'), may hold values from -0.75 to 0.75
- w_up: bfloat16 [1024, 2, 4096], P('dp', None, 'tensor'), may hold values from -0.1875 to 0.1875
- w_down: bfloat16 [1024, 2, 4096], P('dp', None, 'tensor'), may hold values from -0.09375 to 0.09375
- qv_bias: bfloat16 [64, 2, 2, 16], P('dp', None, None, 'tensor'), may hold values from -3 to 3
- up_bias: bfloat16 [64, 2, 64], P('dp', None, 'tensor'), may hold values from -3 to 3
- ln_gain: bfloat16 [1024, 2, 2], P('dp'), may hold values from 0.5 to 1.5
- row_bias: bfloat16 [1024, 2, 4], P('dp'), may hold values from -3 to 3
- cotangent: float32 [20480, 1024], P(('dp', 'tensor')), may hold values from -1.5 to 1.5
Outputs:
- hidden_out: float32 [20480, 1024], P(('dp', 'tensor'))
- grad_in: float32 [20480, 1024], P(('dp', 'tensor'))
- grad_w_qkv: float32 [1024, 2, 3, 1024], P('dp', None, None, 'tensor')
- grad_w_attn_out: float32 [1024, 2, 1024], P('dp', None, 'tensor')
- grad_w_up: float32 [1024, 2, 4096], P('dp', None, 'tensor')
- grad_w_down: float32 [1024, 2, 4096], P('dp', None, 'tensor')
- grad_qv_bias: float32 [64, 2, 2, 16], P('dp', None, None, 'tensor')
- grad_up_bias: float32 [64, 2, 64], P('dp', None, 'tensor')
- grad_ln_gain: float32 [1024, 2, 2], P('dp')
- grad_row_bias: float32 [1024, 2, 4], P('dp')
All inputs are finite; a program needn't handle non-finite values.
Results may differ from a plain program's by a relative error of at most 0.03.
Values may be sent and summed in bfloat16 or wider, within the bound.
No kernel may reach another device: no remote copies, remote signals or barrier semaphores. Data moves between devices by JAX's collectives and lax.ppermute only.
A program may use at most 192 MiB of HBM per device.

v0:
```python
from functools import partial
import jax
import jax.numpy as jnp
from jax import lax
from jax.sharding import Mesh
from jax.sharding import PartitionSpec as P

HEADS = 16
HEAD_DIM = 64
LEN = 160
DP = ("dp_0", "dp_1", "dp_2")
DP_TENSOR = ("dp_0", "dp_1", "dp_2", "tensor")
epsilon = 1e-05


def joined_along(tiles, dim):
    tiles = jnp.moveaxis(tiles, 0, dim)
    shape = tiles.shape
    return tiles.reshape(*shape[:dim], shape[dim] * shape[dim + 1], *shape[dim + 2 :])


def sent_to_all(shard, axis):
    length = lax.axis_size(axis)
    return lax.all_to_all(
        jnp.broadcast_to(shard[None], (length, *shard.shape)), axis, 0, 0, tiled=True
    )


def gather_directly(shard, axis, dim):
    return joined_along(sent_to_all(shard, axis), dim)


def in_one_piece(arrays, axis, dim, along):
    columns = [a.reshape(*a.shape[:along], -1) for a in arrays]
    both = jnp.concatenate(columns, axis=along)
    result, at, outs = (lax.all_gather(both, axis, axis=dim, tiled=True), 0, [])
    for a, column in zip(arrays, columns):
        slab = result[..., at : at + column.shape[along]]
        outs.append(slab.reshape(*slab.shape[:along], *a.shape[along:]))
        at += column.shape[along]
    return tuple(outs)


def side_by_side(arrays, axis, dim, along):
    both = jnp.concatenate(arrays, axis=along)
    result, at, outs = (lax.all_gather(both, axis, axis=dim, tiled=True), 0, [])
    for a in arrays:
        outs.append(lax.slice_in_dim(result, at, at + a.shape[along], axis=along))
        at += a.shape[along]
    return tuple(outs)


def split_up(shard, dim, length):
    before, after = (shard.shape[:dim], shard.shape[dim + 1 :])
    return jnp.moveaxis(shard.reshape(*before, length, -1, *after), dim, 0)


def sent_and_summed(shard, axis, dim):
    tiles = split_up(shard, dim, lax.axis_size(axis))
    arrived = lax.all_to_all(tiles, axis, split_axis=0, concat_axis=0, tiled=True)
    return arrived.astype(jnp.float32).sum(axis=0)


def summed_rows(shard, axes, dim):
    far, near = axes
    own = sent_and_summed(split_up(shard, dim, lax.axis_size(far)), near, dim + 1)
    return jnp.sum(
        lax.all_to_all(own.astype(jnp.bfloat16), far, 0, 0, tiled=True).astype(jnp.float32), axis=0
    )


def in_one_piece_2(arrays, axis, dim, along):
    columns = [a.reshape(*a.shape[:along], -1) for a in arrays]
    both = jnp.concatenate(columns, axis=along)
    result, at, outs = (summed_rows(both, axis, dim), 0, [])
    for a, column in zip(arrays, columns):
        slab = result[..., at : at + column.shape[along]]
        outs.append(slab.reshape(*slab.shape[:along], *a.shape[along:]))
        at += column.shape[along]
    return tuple(outs)


def in_one_piece_3(arrays, axis, dim, along):
    both = jnp.concatenate(arrays, axis=along)
    result, at, outs = (summed_rows(both, axis, dim), 0, [])
    for a in arrays:
        outs.append(lax.slice_in_dim(result, at, at + a.shape[along], axis=along))
        at += a.shape[along]
    return tuple(outs)


def taken_together(shard, axis):
    return sent_to_all(shard, axis).sum(axis=0)


def together(arrays, axis):
    ends = [0]
    for a in arrays:
        ends.append(ends[-1] + a.size)
    so_far = taken_together(jnp.concatenate([a.ravel() for a in arrays]), axis)
    return tuple((so_far[b:e].reshape(a.shape) for a, b, e in zip(arrays, ends, ends[1:])))


def norm_parts(hidden, gain, shift):
    center = jnp.mean(hidden, axis=-1, keepdims=True)
    centered = hidden - center
    variance = jnp.mean(centered * centered, axis=-1, keepdims=True)
    inverse = lax.rsqrt(variance + epsilon)
    normed = centered * inverse
    return (normed, inverse, normed * gain + shift)


def norm_back(upstream, normed, inverse, gain, own_sum):
    scaled = upstream * gain
    center = jnp.mean(scaled, axis=-1, keepdims=True)
    spread = jnp.mean(scaled * normed, axis=-1, keepdims=True)
    result = inverse * (scaled - center - normed * spread)
    return (result, own_sum(upstream * normed), own_sum(upstream))


def alibi_scores(query, keys, slopes):
    length = query.shape[1]
    scores = jnp.einsum(
        "sqhd,skhd->shqk", query, keys, preferred_element_type=jnp.float32
    ) * query.shape[3] ** (-0.5)
    row_index = lax.broadcasted_iota(jnp.int32, (length, length), 0)
    col_index = lax.broadcasted_iota(jnp.int32, (length, length), 1)
    offset = (col_index - row_index).astype(jnp.float32)
    scores = scores + slopes[None, :, None, None] * offset[None, None]
    return jnp.where((col_index <= row_index)[None, None], scores, -jnp.inf)


def attend_forward(query, keys, values, slopes):
    scores = alibi_scores(query, keys, slopes)
    highest = jnp.max(scores, axis=-1, keepdims=True)
    log_total = highest + jnp.log(jnp.sum(jnp.exp(scores - highest), axis=-1, keepdims=True))
    chance = jnp.exp(scores - log_total).astype(jnp.bfloat16)
    context = jnp.einsum("shqk,skhd->sqhd", chance, values, preferred_element_type=jnp.float32)
    return (context.astype(jnp.bfloat16), log_total)


def attend_back(query, keys, values, log_total, d_context, slopes):
    chance = jnp.exp(alibi_scores(query, keys, slopes) - log_total)
    d_value = jnp.einsum(
        "shqk,sqhd->skhd",
        chance.astype(jnp.bfloat16),
        d_context,
        preferred_element_type=jnp.float32,
    )
    d_chance = jnp.einsum("sqhd,skhd->shqk", d_context, values, preferred_element_type=jnp.float32)
    inner_sum = jnp.sum(chance * d_chance, axis=-1, keepdims=True)
    d_scores = (chance * (d_chance - inner_sum) * query.shape[3] ** (-0.5)).astype(jnp.bfloat16)
    d_query = jnp.einsum("shqk,skhd->sqhd", d_scores, keys, preferred_element_type=jnp.float32)
    d_key = jnp.einsum("shqk,sqhd->skhd", d_scores, query, preferred_element_type=jnp.float32)
    return (d_query, d_key, d_value)


def unpack(whole):
    w_mix, w_back, w_raise, w_lower, qv_rows, raise_rows, gains, shifts = whole
    qv_wide = jnp.transpose(qv_rows.astype(jnp.float32), (1, 2, 0)).reshape(2, -1)
    qkv_shift = jnp.stack([qv_wide[0], jnp.zeros_like(qv_wide[0]), qv_wide[1]])
    raise_shift = jnp.transpose(raise_rows.astype(jnp.float32)).reshape(-1)
    return (
        w_mix,
        w_back,
        w_raise,
        w_lower,
        qkv_shift,
        raise_shift,
        gains.astype(jnp.float32),
        shifts.astype(jnp.float32),
    )


def shards(
    hidden_in, w_qkv, w_attn_out, w_up, w_down, qv_bias, up_bias, ln_gain, row_bias, cotangent
):
    own_count = hidden_in.shape[0]
    group_count = own_count * lax.axis_size("tensor")
    layer_count = w_qkv.shape[1]
    local_heads = qv_bias.shape[3]
    head_ids = lax.axis_index("tensor") * local_heads + jnp.arange(local_heads)
    slopes = jnp.exp2(-8.0 * (head_ids.astype(jnp.float32) + 1.0) / HEADS)
    hidden, upstream = (hidden_in, cotangent)

    def own_sum(values):
        return jnp.sum(values, axis=0)

    def spread_rows(values):
        return gather_directly(values, "tensor", 0)

    def spread_grads(values):
        return lax.all_gather(values, "tensor", axis=0, tiled=True)

    def sum_rows(term_fn):
        return lax.psum_scatter(
            term_fn(jnp.int32(0), own_count * lax.axis_size("tensor")).astype(jnp.bfloat16),
            "tensor",
            scatter_dimension=0,
            tiled=True,
        ).astype(jnp.float32)

    def sum_grads(term_fn):
        return lax.psum_scatter(
            term_fn(jnp.int32(0), own_count * lax.axis_size("tensor")).astype(jnp.bfloat16),
            "tensor",
            scatter_dimension=0,
            tiled=True,
        ).astype(jnp.float32)

    kept = []
    stored = []
    for layer_index in range(layer_count):
        whole = (
            *in_one_piece(
                (
                    w_qkv[:, layer_index],
                    w_attn_out[:, layer_index],
                    w_up[:, layer_index],
                    w_down[:, layer_index],
                ),
                DP,
                0,
                1,
            ),
            *in_one_piece((qv_bias[:, layer_index], up_bias[:, layer_index]), DP, 0, 1),
            *side_by_side((ln_gain[:, layer_index], row_bias[:, layer_index]), DP, 0, 1),
        )
        kept.append(whole)
        w_mix, w_back, w_raise, w_lower, qkv_shift, raise_shift, gains, shifts = unpack(whole)
        normed_one, inverse_one, first = norm_parts(hidden, gains[:, 0], shifts[:, 0])
        first_all = spread_rows(first.astype(jnp.bfloat16))
        packed = (
            jnp.einsum("nd,dtc->ntc", first_all, w_mix, preferred_element_type=jnp.float32)
            + qkv_shift
        ).astype(jnp.bfloat16)
        heads = packed.reshape(group_count // LEN, LEN, 3, local_heads, HEAD_DIM)
        context, log_total = attend_forward(heads[:, :, 0], heads[:, :, 1], heads[:, :, 2], slopes)
        context_flat = context.reshape(group_count, -1)

        def attn_term(start, count, context_flat=context_flat, w_back=w_back):
            return jnp.einsum("nc,dc->nd", context_flat, w_back, preferred_element_type=jnp.float32)

        mixed = hidden + sum_rows(attn_term) + shifts[:, 2]
        normed_two, inverse_two, second = norm_parts(mixed, gains[:, 1], shifts[:, 1])
        second_all = spread_rows(second.astype(jnp.bfloat16))
        raised = (
            jnp.einsum("nd,df->nf", second_all, w_raise, preferred_element_type=jnp.float32)
            + raise_shift
        )
        activated = jax.nn.gelu(raised, approximate=True).astype(jnp.bfloat16)

        def feed_term(start, count, activated=activated, w_lower=w_lower):
            return jnp.einsum("nf,df->nd", activated, w_lower, preferred_element_type=jnp.float32)

        hidden = mixed + sum_rows(feed_term) + shifts[:, 3]
        stored.append(
            (
                normed_one,
                inverse_one,
                first_all,
                heads,
                log_total,
                context,
                context_flat,
                normed_two,
                inverse_two,
                second_all,
                raised,
                activated,
            )
        )
    results = [None] * layer_count
    for layer_index in reversed(range(layer_count)):
        whole = kept[layer_index]
        w_mix, w_back, w_raise, w_lower, qkv_shift, raise_shift, gains, shifts = unpack(whole)
        (
            normed_one,
            inverse_one,
            first_all,
            heads,
            log_total,
            context,
            context_flat,
            normed_two,
            inverse_two,
            second_all,
            raised,
            activated,
        ) = stored[layer_index]
        d_out_all = spread_grads(upstream.astype(jnp.bfloat16))
        g_lower_shift = own_sum(upstream)
        d_active = jnp.einsum("nd,df->nf", d_out_all, w_lower, preferred_element_type=jnp.float32)
        unused, pull = jax.vjp(partial(jax.nn.gelu, approximate=True), raised)
        d_raised = pull(d_active)[0]
        d_raised_half = d_raised.astype(jnp.bfloat16)
        g_lower = jnp.einsum("nd,nf->df", d_out_all, activated, preferred_element_type=jnp.float32)
        g_raise = jnp.einsum(
            "nd,nf->df", second_all, d_raised_half, preferred_element_type=jnp.float32
        )
        g_raise_shift = jnp.sum(d_raised, axis=0)

        def feed_back(start, count, d_raised_half=d_raised_half, w_raise=w_raise):
            return jnp.einsum(
                "nf,df->nd", d_raised_half, w_raise, preferred_element_type=jnp.float32
            )

        d_second = sum_grads(feed_back)
        d_norm_two, g_gain_two, g_shift_two = norm_back(
            d_second, normed_two, inverse_two, gains[:, 1], own_sum
        )
        d_mixed = upstream + d_norm_two
        d_mixed_all = spread_grads(d_mixed.astype(jnp.bfloat16))
        g_back_shift = own_sum(d_mixed)
        d_context = jnp.einsum(
            "nd,dc->nc", d_mixed_all, w_back, preferred_element_type=jnp.float32
        ).astype(jnp.bfloat16)
        g_back = jnp.einsum(
            "nd,nc->dc", d_mixed_all, context_flat, preferred_element_type=jnp.float32
        )
        d_query, d_key, d_value = attend_back(
            heads[:, :, 0],
            heads[:, :, 1],
            heads[:, :, 2],
            log_total,
            d_context.reshape(context.shape),
            slopes,
        )
        d_query = d_query.reshape(group_count, -1)
        d_key = d_key.reshape(group_count, -1)
        d_value = d_value.reshape(group_count, -1)
        d_packed = jnp.stack([d_query, d_key, d_value], axis=1).astype(jnp.bfloat16)
        g_mix = jnp.einsum("nd,ntc->dtc", first_all, d_packed, preferred_element_type=jnp.float32)
        g_qv = jnp.stack([jnp.sum(d_query, axis=0), jnp.sum(d_value, axis=0)])

        def attn_back(start, count, d_packed=d_packed, w_mix=w_mix):
            return jnp.einsum("ntc,dtc->nd", d_packed, w_mix, preferred_element_type=jnp.float32)

        d_first = sum_grads(attn_back)
        d_norm_one, g_gain_one, g_shift_one = norm_back(
            d_first, normed_one, inverse_one, gains[:, 0], own_sum
        )
        upstream = d_mixed + d_norm_one
        g_qv_rows = jnp.transpose(g_qv.reshape(2, local_heads, HEAD_DIM), (2, 0, 1))
        g_raise_rows = jnp.transpose(g_raise_shift.reshape(-1, HEAD_DIM))
        g_gains = jnp.stack([g_gain_one, g_gain_two], axis=1)
        g_shifts = jnp.stack([g_shift_one, g_shift_two, g_back_shift, g_lower_shift], axis=1)
        summed = (
            *in_one_piece_2(
                (
                    g_mix.astype(jnp.bfloat16),
                    g_back.astype(jnp.bfloat16),
                    g_raise.astype(jnp.bfloat16),
                    g_lower.astype(jnp.bfloat16),
                ),
                (("dp_0", "dp_1"), "dp_2"),
                0,
                1,
            ),
            *in_one_piece_2(
                (g_qv_rows.astype(jnp.bfloat16), g_raise_rows.astype(jnp.bfloat16)),
                (("dp_0", "dp_1"), "dp_2"),
                0,
                1,
            ),
            *in_one_piece_3(
                (g_gains.astype(jnp.bfloat16), g_shifts.astype(jnp.bfloat16)),
                (("dp_0", "dp_1"), "dp_2"),
                0,
                1,
            ),
        )
        vector_gain, vector_shift = together((summed[6], summed[7]), "tensor")
        results[layer_index] = (
            summed[0],
            summed[1],
            summed[2],
            summed[3],
            summed[4],
            summed[5],
            vector_gain,
            vector_shift,
        )
    stacked = tuple(
        (
            jnp.stack([results[position][member] for position in range(layer_count)], axis=1)
            for member in range(8)
        )
    )
    return (
        hidden,
        upstream,
        stacked[0],
        stacked[1],
        stacked[2],
        stacked[3],
        stacked[4],
        stacked[5],
        stacked[6],
        stacked[7],
    )


def solution(mesh):
    torus = Mesh(
        mesh.devices.reshape(2, 4, 2, mesh.shape["tensor"]), ("dp_0", "dp_1", "dp_2", "tensor")
    )
    placed = (
        P(DP_TENSOR, None),
        P(DP, None, None, "tensor"),
        P(DP, None, "tensor"),
        P(DP, None, "tensor"),
        P(DP, None, "tensor"),
        P(DP, None, None, "tensor"),
        P(DP, None, "tensor"),
        P(DP, None, None),
        P(DP, None, None),
        P(DP_TENSOR, None),
    )
    return jax.shard_map(
        shards,
        mesh=torus,
        in_specs=placed,
        out_specs=(
            P(DP_TENSOR, None),
            P(DP_TENSOR, None),
            P(DP, None, None, "tensor"),
            P(DP, None, "tensor"),
            P(DP, None, "tensor"),
            P(DP, None, "tensor"),
            P(DP, None, None, "tensor"),
            P(DP, None, "tensor"),
            P(DP, None, None),
            P(DP, None, None),
        ),
        check_vma=False,
    )
```

profile of v0, /device:TPU:0, one launch (start us, length us, event | category | flops | bytes accessed | tf_op | source)
XLA Modules:
  0.0 1343.5 jit_solution(9168298569211430551)
XLA Ops:
  15.3 21.1 %all-gather = bf16[16,64,6]{1,2,0:T(8,128)(2,1)S(1)} all-gather(bf16[1,64,6]{1,2,0:T(8,128)(2,1)S(1)} %maximum_bitcast_fusion.3), channel_id=1, replica_groups=mesh['dp_0'=2,'dp_1'=4,'dp_2'=2,'tensor'=8] {'dp_0','dp_1','dp_2'}, dimensions={0}, use_global_device_ids=true | all-gather | bytes 13056 | tf_op jit(solution)/shard_map/all_gather | solution.py:46
  40.2 6.7 all-to-all-start
  47.2 38.4 %all-gather.3 = bf16[16,4,12]{2,1,0:T(4,128)(2,1)S(1)} all-gather(bf16[1,4,12]{2,1,0:T(4,128)(2,1)S(1)} %maximum_bitcast_fusion.6), channel_id=1, replica_groups=mesh['dp_0'=2,'dp_1'=4,'dp_2'=2,'tensor'=8] {'dp_0','dp_1','dp_2'}, dimensions={0}, use_global_device_ids=true | all-gather | bytes 1632 | tf_op jit(solution)/shard_map/all_gather | solution.py:36
  86.0 19.0 %all-gather.1 = bf16[16,4,12]{2,1,0:T(4,128)(2,1)S(1)} all-gather(bf16[1,4,12]{2,1,0:T(4,128)(2,1)S(1)} %maximum_bitcast_fusion.5), channel_id=1, replica_groups=mesh['dp_0'=2,'dp_1'=4,'dp_2'=2,'tensor'=8] {'dp_0','dp_1','dp_2'}, dimensions={0}, use_global_device_ids=true | all-gather | bytes 1632 | tf_op jit(solution)/shard_map/all_gather | solution.py:36
  136.0 80.3 %reduce-scatter.9.cloned.1.call-done = bf16[160,1024]{1,0:T(8,128)(2,1)} async-done(((bf16[1280,1024]{1,0:T(8,128)(2,1)}), bf16[160,1024]{1,0:T(8,128)(2,1)}) %reduce-scatter.9.cloned.1.call-update) | async-done | bytes 327696 | tf_op jit(solution)/shard_map/reduce_scatter | solution.py:196
  229.7 33.0 %all-to-all-done.1 = bf16[8,160,1024]{2,1,0:T(8,128)(2,1)} async-done(((bf16[8,160,1024]{2,1,0:T(8,128)(2,1)}), bf16[8,160,1024]{2,1,0:T(8,128)(2,1)}, u32[]{:S(2)}, u32[]{:S(2)}) %all-to-all-start.1) | async-done | bytes 2621472 | tf_op jit(solution)/shard_map/all_to_all | solution.py:24
  275.7 18.6 %all-gather.2 = bf16[16,64,6]{1,2,0:T(8,128)(2,1)S(1)} all-gather(bf16[1,64,6]{1,2,0:T(8,128)(2,1)S(1)} %maximum_bitcast_fusion.4), channel_id=1, replica_groups=mesh['dp_0'=2,'dp_1'=4,'dp_2'=2,'tensor'=8] {'dp_0','dp_1','dp_2'}, dimensions={0}, use_global_device_ids=true | all-gather | bytes 13056 | tf_op jit(solution)/shard_map/all_gather | solution.py:46
  294.4 52.6 %reduce-scatter.11.cloned.1.call-done = bf16[160,1024]{1,0:T(8,128)(2,1)} async-done(((bf16[1280,1024]{1,0:T(8,128)(2,1)}), bf16[160,1024]{1,0:T(8,128)(2,1)}) %reduce-scatter.11.cloned.1.call-update) | async-done | bytes 327696 | tf_op jit(solution)/shard_map/reduce_scatter | solution.py:196
  355.6 50.2 %all-gather.13.cloned.1.call-done = bf16[1024,1536]{1,0:T(8,128)(2,1)} async-done(((bf16[64,1536]{1,0:T(8,128)(2,1)}), bf16[1024,1536]{1,0:T(8,128)(2,1)}) %all-gather.13.cloned.1.call-update) | async-done | bytes 3145744 | tf_op jit(solution)/shard_map/all_gather | solution.py:36
  439.6 78.0 %reduce-scatter.13.cloned.1.call-done = bf16[160,1024]{1,0:T(8,128)(2,1)} async-done(((bf16[1280,1024]{1,0:T(8,128)(2,1)}), bf16[160,1024]{1,0:T(8,128)(2,1)}) %reduce-scatter.13.cloned.1.call-update) | async-done | bytes 327696 | tf_op jit(solution)/shard_map/reduce_scatter | solution.py:196
  529.8 39.2 %all-to-all-done.3 = bf16[8,160,1024]{2,1,0:T(8,128)(2,1)} async-done(((bf16[8,160,1024]{2,1,0:T(8,128)(2,1)}), bf16[8,160,1024]{2,1,0:T(8,128)(2,1)}, u32[]{:S(2)}, u32[]{:S(2)}) %all-to-all-start.3) | async-done | bytes 2621472 | tf_op jit(solution)/shard_map/all_to_all | solution.py:24
  574.1 27.9 %all-gather.15.cloned.1.call-done = bf16[1280,1024]{1,0:T(8,128)(2,1)} async-done(((bf16[160,1024]{1,0:T(8,128)(2,1)}), bf16[1280,1024]{1,0:T(8,128)(2,1)}) %all-gather.15.cloned.1.call-update) | async-done | bytes 2621456 | tf_op jit(solution)/shard_map/all_gather | solution.py:193
  602.0 5.9 fusion.179
  613.4 5.2 convolution_convert_fusion.2
  618.7 71.8 %reduce-scatter.17.cloned.1.call-done = bf16[160,1024]{1,0:T(8,128)(2,1)} async-done(((bf16[1280,1024]{1,0:T(8,128)(2,1)}), bf16[160,1024]{1,0:T(8,128)(2,1)}) %reduce-scatter.17.cloned.1.call-update) | async-done | bytes 327696 | tf_op jit(solution)/shard_map/reduce_scatter | solution.py:204
  692.2 79.0 %reduce-scatter.15.cloned.1.call-done = bf16[160,1024]{1,0:T(8,128)(2,1)} async-done(((bf16[1280,1024]{1,0:T(8,128)(2,1)}), bf16[160,1024]{1,0:T(8,128)(2,1)}) %reduce-scatter.15.cloned.1.call-update) | async-done | bytes 327696 | tf_op jit(solution)/shard_map/reduce_scatter | solution.py:196
  775.9 57.2 %all-gather.17.cloned.1.call-done = bf16[1280,1024]{1,0:T(8,128)(2,1)} async-done(((bf16[160,1024]{1,0:T(8,128)(2,1)}), bf16[1280,1024]{1,0:T(8,128)(2,1)}) %all-gather.17.cloned.1.call-update) | async-done | bytes 2621456 | tf_op jit(solution)/shard_map/all_gather | solution.py:193
  846.0 6.2 fusion.66
  852.2 6.2 fusion.159
  879.5 77.1 %reduce-scatter.19.cloned.1.call-done = bf16[160,1024]{1,0:T(8,128)(2,1)} async-done(((bf16[1280,1024]{1,0:T(8,128)(2,1)}), bf16[160,1024]{1,0:T(8,128)(2,1)}) %reduce-scatter.19.cloned.1.call-update) | async-done | bytes 327696 | tf_op jit(solution)/shard_map/reduce_scatter | solution.py:204
  961.5 57.8 %all-gather.19.cloned.1.call-done = bf16[1280,1024]{1,0:T(8,128)(2,1)} async-done(((bf16[160,1024]{1,0:T(8,128)(2,1)}), bf16[1280,1024]{1,0:T(8,128)(2,1)}) %all-gather.19.cloned.1.call-update) | async-done | bytes 2621456 | tf_op jit(solution)/shard_map/all_gather | solution.py:193
  1019.3 5.9 fusion.180
  1030.8 76.8 %reduce-scatter.21.cloned.1.call-done = bf16[160,1024]{1,0:T(8,128)(2,1)} async-done(((bf16[1280,1024]{1,0:T(8,128)(2,1)}), bf16[160,1024]{1,0:T(8,128)(2,1)}) %reduce-scatter.21.cloned.1.call-update) | async-done | bytes 327696 | tf_op jit(solution)/shard_map/reduce_scatter | solution.py:204
  1112.6 5.2 fusion.36
  1150.7 10.3 all_to_all.93
  1207.4 5.9 all-to-all-start.7
  1213.3 5.2 convolution_convert_fusion.10
  1241.4 6.6 all-to-all-start.17
  1255.7 10.3 all_to_all.95
  1283.4 17.2 %all-to-all-done.5 = bf16[8,64,1536]{2,1,0:T(8,128)(2,1)} async-done(((bf16[8,64,1536]{2,1,0:T(8,128)(2,1)}), bf16[8,64,1536]{2,1,0:T(8,128)(2,1)}, u32[]{:S(2)}, u32[]{:S(2)}) %all-to-all-start.5) | async-done | bytes 1572896 | tf_op jit(solution)/shard_map/all_to_all | solution.py:68
  1316.8 6.2 all-to-all-done.13
  1329.6 5.5 all-to-all-done.14
  (455 shorter events, 341.5 us)
Async XLA Ops:
  7.2 29.3 %copy-start.1 = (f32[160,1024]{1,0:T(8,128)S(1)}, f32[160,1024]{1,0:T(8,128)}, u32[]{:S(2)}) copy-start(f32[160,1024]{1,0:T(8,128)} %param.10) | copy-start | bytes 1966084
  7.2 100.5 %all-gather.11.cloned.1.call-start = ((), (), s32[]{:S(2)}) async-start(), calls=%async_computation.26 | async-start | bytes 3342336 | tf_op jit(solution)/shard_map/all_gather | solution.py:36
  40.2 69.0 %all-to-all-start = ((bf16[8,160,1024]{2,1,0:T(8,128)(2,1)}), bf16[8,160,1024]{2,1,0:T(8,128)(2,1)}, u32[]{:S(2)}, u32[]{:S(2)}) async-start(bf16[8,160,1024]{2,1,0:T(8,128)(2,1)} %broadcast_in_dim.38), calls=%async_computation | async-start | bytes 5242880 | tf_op jit(solution)/shard_map/all_to_all | solution.py:24
  46.8 169.5 %reduce-scatter.9.cloned.1.call-start = ((), (), s32[]{:S(2)}) async-start(), calls=%async_computation.27 | async-start | bytes 2949120 | tf_op jit(solution)/shard_map/reduce_scatter | solution.py:196
  221.1 41.6 %all-to-all-start.1 = ((bf16[8,160,1024]{2,1,0:T(8,128)(2,1)}), bf16[8,160,1024]{2,1,0:T(8,128)(2,1)}, u32[]{:S(2)}, u32[]{:S(2)}) async-start(bf16[8,160,1024]{2,1,0:T(8,128)(2,1)} %broadcast_in_dim.41), calls=%async_computation.2 | async-start | bytes 5242880 | tf_op jit(solution)/shard_map/all_to_all | solution.py:24
  225.5 121.4 %reduce-scatter.11.cloned.1.call-start = ((), (), s32[]{:S(2)}) async-start(), calls=%async_computation.28 | async-start | bytes 2949120 | tf_op jit(solution)/shard_map/reduce_scatter | solution.py:196
  272.4 133.5 %all-gather.13.cloned.1.call-start = ((), (), s32[]{:S(2)}) async-start(), calls=%async_computation.29 | async-start | bytes 3342336 | tf_op jit(solution)/shard_map/all_gather | solution.py:36
  351.2 59.1 %all-to-all-start.2 = ((bf16[8,160,1024]{2,1,0:T(8,128)(2,1)}), bf16[8,160,1024]{2,1,0:T(8,128)(2,1)}, u32[]{:S(2)}, u32[]{:S(2)}) async-start(bf16[8,160,1024]{2,1,0:T(8,128)(2,1)} %broadcast_in_dim.42), calls=%async_computation.4 | async-start | bytes 5242880 | tf_op jit(solution)/shard_map/all_to_all | solution.py:24
  355.6 54.7 %copy-start.42 = (f32[3,128]{1,0:T(4,128)S(1)}, f32[3,128]{1,0:T(4,128)}, u32[]{:S(2)}) copy-start(f32[3,128]{1,0:T(4,128)} %get-tuple-element.177) | copy-start | bytes 4612
  355.6 162.0 %reduce-scatter.13.cloned.1.call-start = ((), (), s32[]{:S(2)}) async-start(), calls=%async_computation.30 | async-start | bytes 2949120 | tf_op jit(solution)/shard_map/reduce_scatter | solution.py:196
  439.5 162.4 %all-gather.15.cloned.1.call-start = ((), (), s32[]{:S(2)}) async-start(), calls=%async_computation.32 | async-start | bytes 2949120 | tf_op jit(solution)/shard_map/all_gather | solution.py:193
  524.7 44.2 %all-to-all-start.3 = ((bf16[8,160,1024]{2,1,0:T(8,128)(2,1)}), bf16[8,160,1024]{2,1,0:T(8,128)(2,1)}, u32[]{:S(2)}, u32[]{:S(2)}) async-start(bf16[8,160,1024]{2,1,0:T(8,128)(2,1)} %broadcast_in_dim.43), calls=%async_computation.6 | async-start | bytes 5242880 | tf_op jit(solution)/shard_map/all_to_all | solution.py:24
  529.3 161.3 %reduce-scatter.17.cloned.1.call-start = ((), (), s32[]{:S(2)}) async-start(), calls=%async_computation.33 | async-start | bytes 2949120 | tf_op jit(solution)/shard_map/reduce_scatter | solution.py:204
  613.4 157.8 %reduce-scatter.15.cloned.1.call-start = ((), (), s32[]{:S(2)}) async-start(), calls=%async_computation.31 | async-start | bytes 2949120 | tf_op jit(solution)/shard_map/reduce_scatter | solution.py:196
  618.7 214.4 %all-gather.17.cloned.1.call-start = ((), (), s32[]{:S(2)}) async-start(), calls=%async_computation.34 | async-start | bytes 2949120 | tf_op jit(solution)/shard_map/all_gather | solution.py:193
  775.4 181.2 %reduce-scatter.19.cloned.1.call-start = ((), (), s32[]{:S(2)}) async-start(), calls=%async_computation.35 | async-start | bytes 2949120 | tf_op jit(solution)/shard_map/reduce_scatter | solution.py:204
  879.4 139.8 %all-gather.19.cloned.1.call-start = ((), (), s32[]{:S(2)}) async-start(), calls=%async_computation.36 | async-start | bytes 2949120 | tf_op jit(solution)/shard_map/all_gather | solution.py:193
  961.5 146.1 %reduce-scatter.21.cloned.1.call-start = ((), (), s32[]{:S(2)}) async-start(), calls=%async_computation.37 | async-start | bytes 2949120 | tf_op jit(solution)/shard_map/reduce_scatter | solution.py:204
  1030.5 77.1 %copy-start.30 = (f32[1024,1]{0,1:T(1,128)S(1)}, f32[1024,1]{0,1:T(1,128)}, u32[]{:S(2)}) copy-start(f32[1024,1]{0,1:T(1,128)} %get-tuple-element.163) | copy-start | bytes 12292
  1030.5 77.1 %copy-start.34 = (f32[160]{0:T(256)S(1)}, f32[160]{0:T(256)}, u32[]{:S(2)}) copy-start(f32[160]{0:T(256)} %copy-done.33) | copy-start | bytes 1924
  1030.5 77.1 %copy-start.38 = (f32[160]{0:T(256)S(1)}, f32[160]{0:T(256)}, u32[]{:S(2)}) copy-start(f32[160]{0:T(256)} %copy-done.37) | copy-start | bytes 1924
  1030.6 145.5 %all-gather.21.cloned.1.call-start = ((), (), s32[]{:S(2)}) async-start(), calls=%async_computation.38 | async-start | bytes 2949120 | tf_op jit(solution)/shard_map/all_gather | solution.py:193
  1146.1 4.6 all-to-all-start.10
  1161.0 10.6 all-to-all-start.16
  1171.7 35.7 %all-to-all-start.11 = ((bf16[8,4,12]{2,1,0:T(4,128)(2,1)}), bf16[8,4,12]{2,1,0:T(4,128)(2,1)S(1)}, u32[]{:S(2)}, u32[]{:S(2)}) async-start(bf16[8,4,12]{2,1,0:T(4,128)(2,1)} %reduce_sum.518), calls=%async_computation.19 | async-start | bytes 16384 | tf_op jit(solution)/shard_map/all_to_all | solution.py:68
  1176.0 129.9 %reduce-scatter.23.cloned.1.call-start = ((), (), s32[]{:S(2)}) async-start(), calls=%async_computation.39 | async-start | bytes 2949120 | tf_op jit(solution)/shard_map/reduce_scatter | solution.py:204
  1207.4 29.7 %all-to-all-start.7 = ((bf16[8,64,1536]{2,1,0:T(8,128)(2,1)}), bf16[8,64,1536]{2,1,0:T(8,128)(2,1)S(1)}, u32[]{:S(2)}, u32[]{:S(2)}) async-start(bf16[8,64,1536]{2,1,0:T(8,128)(2,1)} %reduce_sum.508), calls=%async_computation.15 | async-start | bytes 3145728 | tf_op jit(solution)/shard_map/all_to_all | solution.py:68
  1241.4 14.3 %all-to-all-start.17 = ((f32[8,1,384]{2,1,0:T(1,128)}), f32[8,1,384]{2,1,0:T(1,128)S(1)}, u32[]{:S(2)}, u32[]{:S(2)}) async-start(f32[8,1,384]{2,1,0:T(1,128)} %broadcast_in_dim.45), calls=%async_computation.25 | async-start | bytes 24576 | tf_op jit(solution)/shard_map/all_to_all | solution.py:24
  1266.0 10.4 all-to-all-start.9
  1276.5 24.1 %all-to-all-start.5 = ((bf16[8,64,1536]{2,1,0:T(8,128)(2,1)}), bf16[8,64,1536]{2,1,0:T(8,128)(2,1)}, u32[]{:S(2)}, u32[]{:S(2)}) async-start(bf16[8,64,1536]{2,1,0:T(8,128)(2,1)} %reduce_sum.506), calls=%async_computation.13 | async-start | bytes 3145728 | tf_op jit(solution)/shard_map/all_to_all | solution.py:68
  1313.1 9.8 all-to-all-start.13
  1324.2 11.0 all-to-all-start.14
  (42 other events, 180.8 us)
Sparse Core Ops, SparseCore 0:
  14.3 53.8 all-gather.10
  136.2 80.1 reduce-scatter.8
  272.5 74.4 reduce-scatter.10
  349.1 56.7 all-gather.12
  439.6 77.9 reduce-scatter.12
  520.4 81.5 all-gather.14
  613.5 77.0 reduce-scatter.16
  694.4 76.6 reduce-scatter.14
  775.5 57.5 all-gather.16
  879.6 76.9 reduce-scatter.18
  961.6 57.6 all-gather.18
  1030.7 76.8 reduce-scatter.20
  1112.6 57.6 all-gather.20
  1207.0 81.7 reduce-scatter.22
where the time goes:
time: 1350 us; the launch traced here: 1340 us
  waiting for transfers between devices  823 us (61%)
  matrix products  138 us (10%)
  blocking collectives  129 us (10%)
  local copies, waits for them, and re-layouts  124 us (9%)
  starting transfers between devices  61.6 us (5%)
  other arithmetic  53.1 us (4%)
  between operations  15.4 us (1%)
    reduce_scatter x4, waiting for transfers between devices, sum_rows(): lax.psum_scatter(term_fn(jnp.int32(0), own_count * lax.axis_size('tensor'...  290 us
    reduce_scatter x4, waiting for transfers between devices, sum_grads(): lax.psum_scatter(term_fn(jnp.int32(0), own_count * lax.axis_size('tensor'...  226 us
    all_gather x4, waiting for transfers between devices, spread_grads(): return lax.all_gather(values, 'tensor', axis=0, tiled=True)  143 us
    all_to_all x6, waiting for transfers between devices, sent_to_all(): lax.all_to_all(jnp.broadcast_to(shard[None], (length, *shard.shape)), axi...  81.6 us
    all_gather x2, blocking collectives, in_one_piece(): result, at, outs = (lax.all_gather(both, axis, axis=dim, tiled=True), 0, [])  57.4 us
    all_gather x2, waiting for transfers between devices, in_one_piece(): result, at, outs = (lax.all_gather(both, axis, axis=dim, tiled=True), 0, [])  50.2 us
    all_gather x2, blocking collectives, side_by_side(): result, at, outs = (lax.all_gather(both, axis, axis=dim, tiled=True), 0, [])  39.7 us
    unnamed x145, local copies, waits for them, and re-layouts  33.6 us
  transfers between devices with their start and end apart: 27, of which 21 were waited for; matrix products, arithmetic and copies ran while one was open for 11% of the time, Pallas kernels for 0%

commit v1 on v0

--- a/solution.py
+++ b/solution.py
@@ -190,7 +190,9 @@
         return gather_directly(values, "tensor", 0)
 
     def spread_grads(values):
-        return lax.all_gather(values, "tensor", axis=0, tiled=True)
+        return jnp.concatenate(
+            lax.all_to_all(jnp.stack([values] * lax.axis_size("tensor")), "tensor", 0, 0), axis=0
+        )
 
     def sum_rows(term_fn):
         return lax.psum_scatter(

time: 1350 us -> 1300 us (0.963)
  waiting for transfers between devices: 823 us -> 663 us
  blocking collectives: 129 us -> 237 us
    all_gather x4 -> x0, waiting for transfers between devices: 143 us -> none  [spread_grads(): return lax.all_gather(values, 'tensor', axis=0, tiled=True)]
    all_to_all x0 -> x3, blocking collectives: none -> 108 us  [the longest x2 72.3 us: spread_grads(): lax.all_to_all(jnp.stack([values] * lax.axis_size('tensor')), 'tensor', 0...]
    all_to_all x0 -> x2, waiting for transfers between devices: none -> 60 us  [spread_grads(): lax.all_to_all(jnp.stack([values] * lax.axis_size('tensor')), 'tensor', 0...]
    reduce_scatter x4, waiting for transfers between devices: 226 us -> 186 us  [sum_grads(): lax.psum_scatter(term_fn(jnp.int32(0), own_count * lax.axis_size('tensor'...]
    all_to_all x6 -> x5, waiting for transfers between devices: 81.6 us -> 42.2 us  [sent_to_all(): lax.all_to_all(jnp.broadcast_to(shard[None], (length, *shard.shape)), axi...]
    all_to_all x6 -> x5, starting transfers between devices: 29.9 us -> 23.1 us  [sent_to_all(): lax.all_to_all(jnp.broadcast_to(shard[None], (length, *shard.shape)), axi...]
    unnamed x145 -> x155, local copies, waits for them, and re-layouts: 33.6 us -> 36.6 us
  transfers between devices with their start and end apart: 27 -> 24, of which waited for: 21 -> 18; matrix products, arithmetic and copies ran while one was open for 11% -> 11% of each run, Pallas kernels for 0% -> 0%
where the time goes in v1:
time: 1300 us; the launch traced here: 1290 us
  waiting for transfers between devices  663 us (51%)
  blocking collectives  237 us (18%)
  matrix products  134 us (10%)
  local copies, waits for them, and re-layouts  131 us (10%)
  starting transfers between devices  63.2 us (5%)
  other arithmetic  48.7 us (4%)
  between operations  15.8 us (1%)
    reduce_scatter x4, waiting for transfers between devices, sum_rows(): lax.psum_scatter(term_fn(jnp.int32(0), own_count * lax.axis_size('tensor'...  291 us
    reduce_scatter x4, waiting for transfers between devices, sum_grads(): lax.psum_scatter(term_fn(jnp.int32(0), own_count * lax.axis_size('tensor'...  186 us
    all_to_all x2, blocking collectives, spread_grads(): lax.all_to_all(jnp.stack([values] * lax.axis_size('tensor')), 'tensor', 0...  72.3 us
    all_to_all x2, waiting for transfers between devices, spread_grads(): lax.all_to_all(jnp.stack([values] * lax.axis_size('tensor')), 'tensor', 0...  60 us
    all_gather x2, blocking collectives, in_one_piece(): result, at, outs = (lax.all_gather(both, axis, axis=dim, tiled=True), 0, [])  57.1 us
    all_gather x2, waiting for transfers between devices, in_one_piece(): result, at, outs = (lax.all_gather(both, axis, axis=dim, tiled=True), 0, [])  50.3 us
    all_to_all x5, waiting for transfers between devices, sent_to_all(): lax.all_to_all(jnp.broadcast_to(shard[None], (length, *shard.shape)), axi...  42.2 us
    all_gather x2, blocking collectives, side_by_side(): result, at, outs = (lax.all_gather(both, axis, axis=dim, tiled=True), 0, [])  39.7 us
  transfers between devices with their start and end apart: 24, of which 18 were waited for; matrix products, arithmetic and copies ran while one was open for 11% of the time, Pallas kernels for 0%

profile of v1, /device:TPU:0, one launch (start us, length us, event | category | flops | bytes accessed | tf_op | source)
XLA Modules:
  0.0 1292.8 jit_solution(5797331509694060087)
XLA Ops:
  15.3 21.1 %all-gather = bf16[16,64,6]{1,2,0:T(8,128)(2,1)S(1)} all-gather(bf16[1,64,6]{1,2,0:T(8,128)(2,1)S(1)} %maximum_bitcast_fusion.3), channel_id=1, replica_groups=mesh['dp_0'=2,'dp_1'=4,'dp_2'=2,'tensor'=8] {'dp_0','dp_1','dp_2'}, dimensions={0}, use_global_device_ids=true | all-gather | bytes 13056 | tf_op jit(solution)/shard_map/all_gather | solution.py:46
  40.3 6.8 all-to-all-start
  47.4 38.1 %all-gather.3 = bf16[16,4,12]{2,1,0:T(4,128)(2,1)S(1)} all-gather(bf16[1,4,12]{2,1,0:T(4,128)(2,1)S(1)} %maximum_bitcast_fusion.6), channel_id=1, replica_groups=mesh['dp_0'=2,'dp_1'=4,'dp_2'=2,'tensor'=8] {'dp_0','dp_1','dp_2'}, dimensions={0}, use_global_device_ids=true | all-gather | bytes 1632 | tf_op jit(solution)/shard_map/all_gather | solution.py:36
  86.5 19.0 %all-gather.1 = bf16[16,4,12]{2,1,0:T(4,128)(2,1)S(1)} all-gather(bf16[1,4,12]{2,1,0:T(4,128)(2,1)S(1)} %maximum_bitcast_fusion.5), channel_id=1, replica_groups=mesh['dp_0'=2,'dp_1'=4,'dp_2'=2,'tensor'=8] {'dp_0','dp_1','dp_2'}, dimensions={0}, use_global_device_ids=true | all-gather | bytes 1632 | tf_op jit(solution)/shard_map/all_gather | solution.py:36
  136.9 80.6 %reduce-scatter.9.cloned.1.call-done = bf16[160,1024]{1,0:T(8,128)(2,1)} async-done(((bf16[1280,1024]{1,0:T(8,128)(2,1)}), bf16[160,1024]{1,0:T(8,128)(2,1)}) %reduce-scatter.9.cloned.1.call-update) | async-done | bytes 327696 | tf_op jit(solution)/shard_map/reduce_scatter | solution.py:198
  230.8 32.7 %all-to-all-done.1 = bf16[8,160,1024]{2,1,0:T(8,128)(2,1)} async-done(((bf16[8,160,1024]{2,1,0:T(8,128)(2,1)}), bf16[8,160,1024]{2,1,0:T(8,128)(2,1)}, u32[]{:S(2)}, u32[]{:S(2)}) %all-to-all-start.1) | async-done | bytes 2621472 | tf_op jit(solution)/shard_map/all_to_all | solution.py:24
  276.5 18.6 %all-gather.2 = bf16[16,64,6]{1,2,0:T(8,128)(2,1)S(1)} all-gather(bf16[1,64,6]{1,2,0:T(8,128)(2,1)S(1)} %maximum_bitcast_fusion.4), channel_id=1, replica_groups=mesh['dp_0'=2,'dp_1'=4,'dp_2'=2,'tensor'=8] {'dp_0','dp_1','dp_2'}, dimensions={0}, use_global_device_ids=true | all-gather | bytes 13056 | tf_op jit(solution)/shard_map/all_gather | solution.py:46
  295.2 52.8 %reduce-scatter.11.cloned.1.call-done = bf16[160,1024]{1,0:T(8,128)(2,1)} async-done(((bf16[1280,1024]{1,0:T(8,128)(2,1)}), bf16[160,1024]{1,0:T(8,128)(2,1)}) %reduce-scatter.11.cloned.1.call-update) | async-done | bytes 327696 | tf_op jit(solution)/shard_map/reduce_scatter | solution.py:198
  356.7 50.2 %all-gather.9.cloned.1.call-done = bf16[1024,1536]{1,0:T(8,128)(2,1)} async-done(((bf16[64,1536]{1,0:T(8,128)(2,1)}), bf16[1024,1536]{1,0:T(8,128)(2,1)}) %all-gather.9.cloned.1.call-update) | async-done | bytes 3145744 | tf_op jit(solution)/shard_map/all_gather | solution.py:36
  440.7 78.3 %reduce-scatter.13.cloned.1.call-done = bf16[160,1024]{1,0:T(8,128)(2,1)} async-done(((bf16[1280,1024]{1,0:T(8,128)(2,1)}), bf16[160,1024]{1,0:T(8,128)(2,1)}) %reduce-scatter.13.cloned.1.call-update) | async-done | bytes 327696 | tf_op jit(solution)/shard_map/reduce_scatter | solution.py:198
  522.1 35.9 %all_to_all.112 = bf16[8,160,1024]{2,1,0:T(8,128)(2,1)} all-to-all(bf16[8,160,1024]{2,1,0:T(8,128)(2,1)S(1)} %broadcast_in_dim.43), channel_id=1, replica_groups=mesh['dp_0'=2,'dp_1'=4,'dp_2'=2,'tensor'=8] {'tensor'}, dimensions={0} | all-to-all | bytes 5242880 | tf_op jit(solution)/shard_map/all_to_all | solution.py:24
  570.0 28.2 %all-to-all-done.4 = bf16[8,160,1024]{2,1,0:T(8,128)(2,1)} async-done(((bf16[8,160,1024]{2,1,0:T(8,128)(2,1)}), bf16[8,160,1024]{2,1,0:T(8,128)(2,1)}, u32[]{:S(2)}, u32[]{:S(2)}) %all-to-all-start.4) | async-done | bytes 2621472 | tf_op jit(solution)/shard_map/all_to_all | solution.py:194
  598.2 5.9 fusion.179
  609.6 5.2 convolution_convert_fusion.2
  614.9 70.3 %reduce-scatter.17.cloned.1.call-done = bf16[160,1024]{1,0:T(8,128)(2,1)} async-done(((bf16[1280,1024]{1,0:T(8,128)(2,1)}), bf16[160,1024]{1,0:T(8,128)(2,1)}) %reduce-scatter.17.cloned.1.call-update) | async-done | bytes 327696 | tf_op jit(solution)/shard_map/reduce_scatter | solution.py:206
  686.8 79.0 %reduce-scatter.15.cloned.1.call-done = bf16[160,1024]{1,0:T(8,128)(2,1)} async-done(((bf16[1280,1024]{1,0:T(8,128)(2,1)}), bf16[160,1024]{1,0:T(8,128)(2,1)}) %reduce-scatter.15.cloned.1.call-update) | async-done | bytes 327696 | tf_op jit(solution)/shard_map/reduce_scatter | solution.py:198
  769.6 36.2 %all_to_all.113 = bf16[8,160,1024]{2,1,0:T(8,128)(2,1)S(1)} all-to-all(bf16[8,160,1024]{2,1,0:T(8,128)(2,1)S(1)} %stack.167), channel_id=1, replica_groups=mesh['dp_0'=2,'dp_1'=4,'dp_2'=2,'tensor'=8] {'tensor'}, dimensions={0} | all-to-all | bytes 5242880 | tf_op jit(solution)/shard_map/all_to_all | solution.py:194
  819.4 6.7 fusion.66
  826.2 6.6 fusion.159
  853.9 76.7 %reduce-scatter.19.cloned.1.call-done = bf16[160,1024]{1,0:T(8,128)(2,1)} async-done(((bf16[1280,1024]{1,0:T(8,128)(2,1)}), bf16[160,1024]{1,0:T(8,128)(2,1)}) %reduce-scatter.19.cloned.1.call-update) | async-done | bytes 327696 | tf_op jit(solution)/shard_map/reduce_scatter | solution.py:206
  935.1 36.1 %all_to_all.114 = bf16[8,160,1024]{2,1,0:T(8,128)(2,1)S(1)} all-to-all(bf16[8,160,1024]{2,1,0:T(8,128)(2,1)S(1)} %stack.169), channel_id=1, replica_groups=mesh['dp_0'=2,'dp_1'=4,'dp_2'=2,'tensor'=8] {'tensor'}, dimensions={0} | all-to-all | bytes 5242880 | tf_op jit(solution)/shard_map/all_to_all | solution.py:194
  1016.4 39.2 %reduce-scatter.21.cloned.1.call-done = bf16[160,1024]{1,0:T(8,128)(2,1)} async-done(((bf16[1280,1024]{1,0:T(8,128)(2,1)}), bf16[160,1024]{1,0:T(8,128)(2,1)}) %reduce-scatter.21.cloned.1.call-update) | async-done | bytes 327696 | tf_op jit(solution)/shard_map/reduce_scatter | solution.py:206
  1057.2 10.4 all_to_all.116
  1081.1 5.4 all-to-all-start.7
  1091.5 31.8 %all-to-all-done.7 = bf16[8,160,1024]{2,1,0:T(8,128)(2,1)} async-done(((bf16[8,160,1024]{2,1,0:T(8,128)(2,1)}), bf16[8,160,1024]{2,1,0:T(8,128)(2,1)}, u32[]{:S(2)}, u32[]{:S(2)}) %all-to-all-start.7) | async-done | bytes 2621472 | tf_op jit(solution)/shard_map/all_to_all | solution.py:194
  1158.4 6.0 all-to-all-start.11
  1164.3 5.4 convolution_convert_fusion.10
  1183.4 5.2 all-to-all-done.11
  1203.8 10.4 all_to_all.118
  1231.3 17.2 %all-to-all-done.9 = bf16[8,64,1536]{2,1,0:T(8,128)(2,1)} async-done(((bf16[8,64,1536]{2,1,0:T(8,128)(2,1)}), bf16[8,64,1536]{2,1,0:T(8,128)(2,1)}, u32[]{:S(2)}, u32[]{:S(2)}) %all-to-all-start.9) | async-done | bytes 1572896 | tf_op jit(solution)/shard_map/all_to_all | solution.py:68
  1264.7 6.2 all-to-all-done.17
  1278.4 5.6 all-to-all-done.18
  (462 shorter events, 349.1 us)
Async XLA Ops:
  7.2 29.4 %copy-start.1 = (f32[160,1024]{1,0:T(8,128)S(1)}, f32[160,1024]{1,0:T(8,128)}, u32[]{:S(2)}) copy-start(f32[160,1024]{1,0:T(8,128)} %param.10) | copy-start | bytes 1966084
  7.2 101.4 %all-gather.7.cloned.1.call-start = ((), (), s32[]{:S(2)}) async-start(), calls=%async_computation.30 | async-start | bytes 3342336 | tf_op jit(solution)/shard_map/all_gather | solution.py:36
  40.3 69.8 %all-to-all-start = ((bf16[8,160,1024]{2,1,0:T(8,128)(2,1)}), bf16[8,160,1024]{2,1,0:T(8,128)(2,1)}, u32[]{:S(2)}, u32[]{:S(2)}) async-start(bf16[8,160,1024]{2,1,0:T(8,128)(2,1)} %broadcast_in_dim.38), calls=%async_computation | async-start | bytes 5242880 | tf_op jit(solution)/shard_map/all_to_all | solution.py:24
  47.0 170.4 %reduce-scatter.9.cloned.1.call-start = ((), (), s32[]{:S(2)}) async-start(), calls=%async_computation.31 | async-start | bytes 2949120 | tf_op jit(solution)/shard_map/reduce_scatter | solution.py:198
  222.2 41.3 %all-to-all-start.1 = ((bf16[8,160,1024]{2,1,0:T(8,128)(2,1)}), bf16[8,160,1024]{2,1,0:T(8,128)(2,1)}, u32[]{:S(2)}, u32[]{:S(2)}) async-start(bf16[8,160,1024]{2,1,0:T(8,128)(2,1)} %broadcast_in_dim.41), calls=%async_computation.2 | async-start | bytes 5242880 | tf_op jit(solution)/shard_map/all_to_all | solution.py:24
  226.6 121.4 %reduce-scatter.11.cloned.1.call-start = ((), (), s32[]{:S(2)}) async-start(), calls=%async_computation.32 | async-start | bytes 2949120 | tf_op jit(solution)/shard_map/reduce_scatter | solution.py:198
  273.2 133.8 %all-gather.9.cloned.1.call-start = ((), (), s32[]{:S(2)}) async-start(), calls=%async_computation.33 | async-start | bytes 3342336 | tf_op jit(solution)/shard_map/all_gather | solution.py:36
  352.3 59.1 %all-to-all-start.2 = ((bf16[8,160,1024]{2,1,0:T(8,128)(2,1)}), bf16[8,160,1024]{2,1,0:T(8,128)(2,1)}, u32[]{:S(2)}, u32[]{:S(2)}) async-start(bf16[8,160,1024]{2,1,0:T(8,128)(2,1)} %broadcast_in_dim.42), calls=%async_computation.4 | async-start | bytes 5242880 | tf_op jit(solution)/shard_map/all_to_all | solution.py:24
  356.7 54.7 %copy-start.46 = (f32[3,128]{1,0:T(4,128)S(1)}, f32[3,128]{1,0:T(4,128)}, u32[]{:S(2)}) copy-start(f32[3,128]{1,0:T(4,128)} %get-tuple-element.177) | copy-start | bytes 4612
  356.7 162.3 %reduce-scatter.13.cloned.1.call-start = ((), (), s32[]{:S(2)}) async-start(), calls=%async_computation.34 | async-start | bytes 2949120 | tf_op jit(solution)/shard_map/reduce_scatter | solution.py:198
  559.8 38.4 %all-to-all-start.4 = ((bf16[8,160,1024]{2,1,0:T(8,128)(2,1)}), bf16[8,160,1024]{2,1,0:T(8,128)(2,1)}, u32[]{:S(2)}, u32[]{:S(2)}) async-start(bf16[8,160,1024]{2,1,0:T(8,128)(2,1)} %stack.166), calls=%async_computation.8 | async-start | bytes 5242880 | tf_op jit(solution)/shard_map/all_to_all | solution.py:194
  564.4 120.8 %reduce-scatter.17.cloned.1.call-start = ((), (), s32[]{:S(2)}) async-start(), calls=%async_computation.36 | async-start | bytes 2949120 | tf_op jit(solution)/shard_map/reduce_scatter | solution.py:206
  609.5 156.2 %reduce-scatter.15.cloned.1.call-start = ((), (), s32[]{:S(2)}) async-start(), calls=%async_computation.35 | async-start | bytes 2949120 | tf_op jit(solution)/shard_map/reduce_scatter | solution.py:198
  614.8 315.7 %reduce-scatter.19.cloned.1.call-start = ((), (), s32[]{:S(2)}) async-start(), calls=%async_computation.37 | async-start | bytes 2949120 | tf_op jit(solution)/shard_map/reduce_scatter | solution.py:206
  853.8 201.8 %reduce-scatter.21.cloned.1.call-start = ((), (), s32[]{:S(2)}) async-start(), calls=%async_computation.38 | async-start | bytes 2949120 | tf_op jit(solution)/shard_map/reduce_scatter | solution.py:206
  934.8 36.5 %copy-start.49 = (f32[1280,512]{1,0:T(8,128)S(1)}, f32[1280,512]{1,0:T(8,128)}, u32[]{:S(2)}) copy-start(f32[1280,512]{1,0:T(8,128)} %copy-done.48) | copy-start | bytes 7864324
  935.1 36.1 %copy-start.25 = (bf16[1024,1536]{1,0:T(8,128)(2,1)S(1)}, bf16[1024,1536]{1,0:T(8,128)(2,1)}, u32[]{:S(2)}) copy-start(bf16[1024,1536]{1,0:T(8,128)(2,1)} %all-gather.7.cloned.1.call-done) | copy-start | bytes 9437188
  1005.3 50.4 %copy-start.34 = (f32[1024,1]{0,1:T(1,128)S(1)}, f32[1024,1]{0,1:T(1,128)}, u32[]{:S(2)}) copy-start(f32[1024,1]{0,1:T(1,128)} %get-tuple-element.163) | copy-start | bytes 12292
  1005.3 50.3 %copy-start.38 = (f32[160]{0:T(256)S(1)}, f32[160]{0:T(256)}, u32[]{:S(2)}) copy-start(f32[160]{0:T(256)} %copy-done.37) | copy-start | bytes 1924
  1005.3 50.3 %copy-start.42 = (f32[160]{0:T(256)S(1)}, f32[160]{0:T(256)}, u32[]{:S(2)}) copy-start(f32[160]{0:T(256)} %copy-done.41) | copy-start | bytes 1924
  1012.4 44.8 %all-to-all-start.14 = ((bf16[2,2,192]{2,1,0:T(2,128)(2,1)}), bf16[2,2,192]{2,1,0:T(2,128)(2,1)S(1)}, u32[]{:S(2)}, u32[]{:S(2)}) async-start(bf16[2,2,192]{2,1,0:T(2,128)(2,1)} %reshape.434), calls=%async_computation.22 | async-start | bytes 4096 | tf_op jit(solution)/shard_map/all_to_all | solution.py:60
  1067.6 10.6 all-to-all-start.20
  1081.1 42.2 %all-to-all-start.7 = ((bf16[8,160,1024]{2,1,0:T(8,128)(2,1)}), bf16[8,160,1024]{2,1,0:T(8,128)(2,1)}, u32[]{:S(2)}, u32[]{:S(2)}) async-start(bf16[8,160,1024]{2,1,0:T(8,128)(2,1)} %stack.170), calls=%async_computation.14 | async-start | bytes 5242880 | tf_op jit(solution)/shard_map/all_to_all | solution.py:194
  1123.3 35.1 %all-to-all-start.15 = ((bf16[8,4,12]{2,1,0:T(4,128)(2,1)}), bf16[8,4,12]{2,1,0:T(4,128)(2,1)S(1)}, u32[]{:S(2)}, u32[]{:S(2)}) async-start(bf16[8,4,12]{2,1,0:T(4,128)(2,1)} %reduce_sum.518), calls=%async_computation.23 | async-start | bytes 16384 | tf_op jit(solution)/shard_map/all_to_all | solution.py:68
  1127.0 126.8 %reduce-scatter.23.cloned.1.call-start = ((), (), s32[]{:S(2)}) async-start(), calls=%async_computation.39 | async-start | bytes 2949120 | tf_op jit(solution)/shard_map/reduce_scatter | solution.py:206
  1158.4 30.2 %all-to-all-start.11 = ((bf16[8,64,1536]{2,1,0:T(8,128)(2,1)}), bf16[8,64,1536]{2,1,0:T(8,128)(2,1)S(1)}, u32[]{:S(2)}, u32[]{:S(2)}) async-start(bf16[8,64,1536]{2,1,0:T(8,128)(2,1)} %reduce_sum.508), calls=%async_computation.19 | async-start | bytes 3145728 | tf_op jit(solution)/shard_map/all_to_all | solution.py:68
  1192.9 11.0 all-to-all-start.21
  1214.2 10.2 all-to-all-start.13
  1224.4 24.1 %all-to-all-start.9 = ((bf16[8,64,1536]{2,1,0:T(8,128)(2,1)}), bf16[8,64,1536]{2,1,0:T(8,128)(2,1)}, u32[]{:S(2)}, u32[]{:S(2)}) async-start(bf16[8,64,1536]{2,1,0:T(8,128)(2,1)} %reduce_sum.506), calls=%async_computation.17 | async-start | bytes 3145728 | tf_op jit(solution)/shard_map/all_to_all | solution.py:68
  1251.0 25.3 %copy-start.6 = (f32[160,1024]{1,0:T(8,128)S(1)}, f32[160,1024]{1,0:T(8,128)}, u32[]{:S(2)}) copy-start(f32[160,1024]{1,0:T(8,128)} %copy-done.5) | copy-start | bytes 1966084
  1261.1 9.8 all-to-all-start.17
  1272.1 11.9 all-to-all-start.18
  (44 other events, 138.5 us)
Sparse Core Ops, SparseCore 0:
  14.3 54.0 all-gather.6
  137.0 80.4 reduce-scatter.8
  273.3 74.6 reduce-scatter.10
  350.1 56.8 all-gather.8
  440.8 78.1 reduce-scatter.12
  609.7 75.4 reduce-scatter.16
  689.0 76.7 reduce-scatter.14
  854.0 76.5 reduce-scatter.18
  978.7 76.8 reduce-scatter.20
  1158.0 81.3 reduce-scatter.22
